TPU v7x, 32 devices: a whole 2x2x4 slice. The times are simulated.
32 devices in a mesh: grp: 2 (over x), row: 16 (over z, y, core).
Axes of the slice: x: 2, y: 2, z: 4, core: 2. Of those that a mesh axis runs over, the one named last changes fastest.
Arguments:
- pair_map: bfloat16 [256, 128, 128], P(('grp', 'row')), parts along dimension 0, may hold values from -6 to 6
- norm_gain: float32 [128], replicated, may hold values from 0.1 to 1.9
- w_query: bfloat16 [128, 128], replicated, may hold values from -30 to 30
- w_key: bfloat16 [128, 128], replicated, may hold values from -1 to 1
- w_value: bfloat16 [128, 128], replicated, may hold values from -0.5 to 0.5
- w_gate: bfloat16 [128, 128], replicated, may hold values from -0.5 to 0.5
- w_bias: bfloat16 [128, 4], replicated, may hold values from -12 to 12
- w_output: bfloat16 [128, 128], replicated, may hold values from -0.5 to 0.5
- window_start: int32 [256], P(('grp', 'row')), parts along dimension 0, may hold values from 0 to 63
- key_length: int32 [256], P(('grp', 'row')), parts along dimension 0, may hold values from 32 to 64
Outputs:
- update: bfloat16 [256, 128, 128], P('grp', 'row'), parts along dimension 0
There are 2 independent parts, one for each index of `grp`. A program takes and returns all parts, laid end to end along the dimension named above; an argument that names none is the same for every part. Nothing has to cross between parts.
All inputs are finite; a program needn't handle non-finite values.
Results may differ from a plain program's by a relative error of at most 0.0025.
The roundings to bfloat16 on the way count: a program that leaves them out, or rounds other values in their place, can miss the bound.
Values may be sent and summed in bfloat16 or wider, within the bound.
A program may use at most 128 MiB of HBM per device.

v0:
```python
import math

import jax
import jax.numpy as jnp
from jax import lax
from jax.sharding import PartitionSpec as P

H = 4


def normalize(rows, norm_gain):
    values = rows.astype(jnp.float32)
    center = jnp.mean(values, axis=-1, keepdims=True)
    spread = jnp.mean((values - center) ** 2, axis=-1, keepdims=True)
    return ((values - center) * lax.rsqrt(spread + 1e-05) * norm_gain).astype(jnp.bfloat16)


def local(
    pair_map, norm_gain, w_query, w_key, w_value, w_gate, w_bias, w_output, window_start, key_length
):
    rows, width, channels = pair_map.shape
    head_size = channels // H
    normed = normalize(pair_map, norm_gain)
    stacked = jnp.concatenate([w_query, w_key, w_value, w_gate], axis=1)
    projected = jnp.dot(
        normed.reshape(rows * width, channels), stacked, preferred_element_type=jnp.float32
    )
    query = projected[:, :channels].astype(jnp.bfloat16).reshape(rows, width, H, head_size)
    key = (
        projected[:, channels : 2 * channels]
        .astype(jnp.bfloat16)
        .reshape(rows, width, H, head_size)
    )
    value = (
        projected[:, 2 * channels : 3 * channels]
        .astype(jnp.bfloat16)
        .reshape(rows, width, H, head_size)
    )
    gate = projected[:, 3 * channels :].astype(jnp.bfloat16).reshape(rows, width, channels)
    local_bias = jnp.einsum("rnc,ch->hrn", normed, w_bias, preferred_element_type=jnp.float32)
    positions = jnp.arange(width, dtype=jnp.int32)
    valid = (positions[None, :] >= window_start[:, None]) & (
        positions[None, :] < (window_start + key_length)[:, None]
    )
    factor = 1.0 / head_size**0.5
    all_bias = lax.all_gather(local_bias, "row", axis=1, tiled=True)
    length = all_bias.shape[1]
    block = math.gcd(length, 64)

    def one_block(index):
        offset = index * block
        bias_block = lax.dynamic_slice_in_dim(all_bias, offset, block, 1)
        query_block = lax.dynamic_slice_in_dim(query, offset, block, 1)
        gate_block = lax.dynamic_slice_in_dim(gate, offset, block, 1)
        scores = (
            jnp.einsum("rjhd,rkhd->rhjk", query_block, key, preferred_element_type=jnp.float32)
            * factor
        )
        scores = scores + bias_block[None]
        scores = jnp.where(valid[:, None, None, :], scores, jnp.float32(-1e30))
        top = jnp.max(scores, axis=-1, keepdims=True)
        raised = jnp.exp(scores - top)
        weights = (raised / jnp.sum(raised, axis=-1, keepdims=True)).astype(jnp.bfloat16)
        attended = jnp.einsum("rhjk,rkhd->rjhd", weights, value, preferred_element_type=jnp.float32)
        attended = attended.reshape(rows, block, channels)
        gated = (jax.nn.sigmoid(gate_block.astype(jnp.float32)) * attended).astype(jnp.bfloat16)
        mixed = jnp.dot(
            gated.reshape(rows * block, channels), w_output, preferred_element_type=jnp.float32
        )
        return mixed.astype(jnp.bfloat16).reshape(rows, block, channels)

    blocks = lax.map(one_block, jnp.arange(length // block, dtype=jnp.int32))
    result = jnp.moveaxis(blocks, 0, 1).reshape(rows, length, channels)
    return lax.all_to_all(result, "row", split_axis=1, concat_axis=0, tiled=True)


def solution(mesh):
    return jax.shard_map(
        local,
        mesh=mesh,
        in_specs=(
            P(("grp", "row"), None, None),
            P(),
            P(),
            P(),
            P(),
            P(),
            P(),
            P(),
            P(("grp", "row")),
            P(("grp", "row")),
        ),
        out_specs=P("grp", "row", None),
        check_vma=False,
    )
```

profile of v0, /device:TPU:0, one launch (start us, length us, event | category | flops | bytes accessed | tf_op | source)
XLA Modules:
  0.0 56.8 jit_solution(8926814176208976086)
XLA Ops:
  0.0 0.0 copy-start
  0.0 0.0 copy-start.5
  0.0 0.0 copy-start.4
  0.0 0.0 copy-start.3
  0.0 0.0 copy-start.2
  0.0 1.1 %convert_reduce_fusion = f32[8,128]{1,0:T(8,128)S(1)} fusion(bf16[8,128,128]{2,1,0:T(8,128)(2,1)} %param.12), kind=kLoop, calls=%fused_computation.24 | loop fusion | flops 261120 | bytes 266240 | tf_op jit(solution)/shard_map/reduce_sum | solution.py:13
  1.2 1.3 %fusion.17 = f32[8,128]{1,0:T(8,128)S(1)} fusion(bf16[8,128,128]{2,1,0:T(8,128)(2,1)} %param.12, f32[8,128]{1,0:T(8,128)S(1)} %broadcast_multiply_fusion), kind=kLoop, calls=%fused_computation.27 | loop fusion | flops 523264 | bytes 270336 | tf_op jit(solution)/shard_map/reduce_sum | solution.py:14
  2.5 1.3 %fusion.19 = bf16[8,128,128]{2,1,0:T(8,128)(2,1)S(1)} fusion(bf16[8,128,128]{2,1,0:T(8,128)(2,1)} %param.12, f32[128]{0:T(128)} %param.13, f32[8,128]{1,0:T(8,128)S(1)} %add_rsqrt_fusion, f32[8,128]{1,0:T(8,128)S(1)} %broadcast_multiply_fusion), kind=kLoop, calls=%fused_computation.29 | loop fusion | flops 655360 | bytes 532992 | tf_op jit(solution)/shard_map/convert_element_type | solution.py:15
  3.8 0.0 copy-done.5
  3.8 0.0 copy-done.4
  3.8 0.0 copy-done.3
  3.9 0.0 copy-done.2
  3.9 0.4 convolution_convert_fusion.1
  4.3 0.2 fusion.32
  4.5 0.1 copy.37
  4.7 0.1 copy.38
  4.9 0.0 copy-start.6
  4.9 0.0 copy-start.7
  5.0 0.0 copy-start.1
  5.0 0.1 copy.36
  5.2 0.0 copy-done
  5.2 0.2 convolution_bitcast_fusion
  5.4 23.8 %all_gather.3 = f32[4,128,128]{2,0,1:T(4,128)S(1)} all-gather(f32[4,8,128]{2,0,1:T(4,128)S(1)} %convolution_bitcast_fusion), channel_id=1, replica_groups=mesh['grp'=2,'row'=16] {'row'}, dimensions={1}, use_global_device_ids=true | all-gather | bytes 278528 | tf_op jit(solution)/shard_map/all_gather | solution.py:46
  29.2 0.0 copy-done.6
  29.2 0.0 copy-done.7
  29.2 0.0 copy-done.1
  29.3 13.9 %while.11 = (s32[]{:T(128)}, bf16[2,8,64,128]{3,2,0,1:T(8,128)(2,1)S(1)}, s32[2]{0:T(128)S(1)}, bf16[8,128,128]{2,1,0:T(8,128)(2,1)S(1)}, bf16[8,128,4,32]{1,0,3...) while((s32[]{:T(128)}, ...), condition=%wide.region_5.6_spmd.clone, body=%wide.region_2.5_spmd.clone.sunk | while | flops 70456576 | bytes 6081815 | solution.py:72
  29.3 0.7 %dynamic_slice.27 = s32[1]{0:T(128)} dynamic-slice(s32[2]{0:T(128)S(1)} %get-tuple-element.253, s32[]{:T(128)} %get-tuple-element.236), dynamic_slice_sizes={1} | dynamic-slice | bytes 12 | tf_op jit(solution)/shard_map/while/body/jit(dynamic_index_in_dim)/dynamic_slice | solution.py:72
  30.6 0.1 constant_dynamic-slice_fusion.5
  30.8 0.1 fusion.61
  30.9 0.3 fusion.63
  31.3 0.8 %fusion.62 = f32[8,4,64]{2,1,0:T(4,128)S(1)} fusion(bf16[8,128,4,32]{1,3,2,0:T(8,128)(2,1)S(1)} %get-tuple-element.256, f32[4,64,128]{2,1,0:T(8,128)S(1)} %copy.67, pred[8,128]{1,0:T(8,128)(4,1)S(1)} %fusion.61, bf16[8,64,4,32]{1,0,3,2:T(8,128)(2,1)S(1)} %constant_dynamic-slice_fusion.5), kind=kOutput, calls=%fused_computation.41.clone.1 | convolution fusion | flops 18088064 | bytes 533504 | tf_op jit(solution)/shard_map/while/body/eval_jaxpr/sub | solution.py:62
  32.1 3.6 %fusion.64 = f32[8,4,64,32]{2,3,1,0:T(8,128)S(1)} fusion(bf16[8,128,4,32]{1,3,2,0:T(8,128)(2,1)S(1)} %get-tuple-element.258, f32[8,4,64]{2,1,0:T(4,128)S(1)} %fusion.62, f32[8,4,64,128]{3,2,1,0:T(8,128)S(1)} %fusion.63), kind=kOutput, calls=%fused_computation.9.clone.1 | convolution fusion | flops 17565824 | bytes 1581056 | tf_op jit(solution)/shard_map/while/body/eval_jaxpr/rhjk,rkhd->rjhd/dot_general | solution.py:64
  35.7 0.2 copy.68
  35.9 0.1 multiply_convert_fusion.2
  36.0 0.2 convolution_convert_fusion.3
  36.2 0.7 %dynamic_slice.27 = s32[1]{0:T(128)} dynamic-slice(s32[2]{0:T(128)S(1)} %get-tuple-element.253, s32[]{:T(128)} %get-tuple-element.236), dynamic_slice_sizes={1} | dynamic-slice | bytes 12 | tf_op jit(solution)/shard_map/while/body/jit(dynamic_index_in_dim)/dynamic_slice | solution.py:72
  37.6 0.1 constant_dynamic-slice_fusion.5
  37.8 0.1 fusion.61
  37.9 0.3 fusion.63
  38.2 0.8 %fusion.62 = f32[8,4,64]{2,1,0:T(4,128)S(1)} fusion(bf16[8,128,4,32]{1,3,2,0:T(8,128)(2,1)S(1)} %get-tuple-element.256, f32[4,64,128]{2,1,0:T(8,128)S(1)} %copy.67, pred[8,128]{1,0:T(8,128)(4,1)S(1)} %fusion.61, bf16[8,64,4,32]{1,0,3,2:T(8,128)(2,1)S(1)} %constant_dynamic-slice_fusion.5), kind=kOutput, calls=%fused_computation.41.clone.1 | convolution fusion | flops 18088064 | bytes 533504 | tf_op jit(solution)/shard_map/while/body/eval_jaxpr/sub | solution.py:62
  39.1 3.6 %fusion.64 = f32[8,4,64,32]{2,3,1,0:T(8,128)S(1)} fusion(bf16[8,128,4,32]{1,3,2,0:T(8,128)(2,1)S(1)} %get-tuple-element.258, f32[8,4,64]{2,1,0:T(4,128)S(1)} %fusion.62, f32[8,4,64,128]{3,2,1,0:T(8,128)S(1)} %fusion.63), kind=kOutput, calls=%fused_computation.9.clone.1 | convolution fusion | flops 17565824 | bytes 1581056 | tf_op jit(solution)/shard_map/while/body/eval_jaxpr/rhjk,rkhd->rjhd/dot_general | solution.py:64
  42.7 0.2 copy.68
  42.9 0.1 multiply_convert_fusion.2
  43.0 0.2 convolution_convert_fusion.3
  43.2 0.2 copy.44
  43.4 12.6 %all_to_all.18 = bf16[8,128,128]{2,0,1:T(8,128)(2,1)S(1)} all-to-all(bf16[8,128,128]{2,0,1:T(8,128)(2,1)S(1)} %copy.44), channel_id=1, replica_groups=mesh['grp'=2,'row'=16] {'row'}, dimensions={1} | all-to-all | bytes 524288 | tf_op jit(solution)/shard_map/all_to_all | solution.py:74
  56.0 0.8 %copy.46 = bf16[16,8,8,128]{3,2,1,0:T(8,128)(2,1)} copy(bf16[16,8,8,128]{3,1,2,0:T(8,128)(2,1)S(1)} %bitcast.76) | data formatting | bytes 524288 | tf_op jit(solution)/shard_map/all_to_all | solution.py:74
  (16 shorter events, 0.3 us)
Async XLA Ops:
  0.0 5.2 %copy-start = (bf16[128,4]{0,1:T(4,128)(2,1)S(1)}, bf16[128,4]{0,1:T(4,128)(2,1)}, u32[]{:S(2)}) copy-start(bf16[128,4]{0,1:T(4,128)(2,1)} %param.18) | copy-start | bytes 3076
  0.0 3.8 %copy-start.5 = (bf16[128,128]{1,0:T(8,128)(2,1)S(1)}, bf16[128,128]{1,0:T(8,128)(2,1)}, u32[]{:S(2)}) copy-start(bf16[128,128]{1,0:T(8,128)(2,1)} %param.14) | copy-start | bytes 98308
  0.0 3.8 %copy-start.4 = (bf16[128,128]{1,0:T(8,128)(2,1)S(1)}, bf16[128,128]{1,0:T(8,128)(2,1)}, u32[]{:S(2)}) copy-start(bf16[128,128]{1,0:T(8,128)(2,1)} %param.15) | copy-start | bytes 98308
  0.0 3.8 %copy-start.3 = (bf16[128,128]{1,0:T(8,128)(2,1)S(1)}, bf16[128,128]{1,0:T(8,128)(2,1)}, u32[]{:S(2)}) copy-start(bf16[128,128]{1,0:T(8,128)(2,1)} %param.16) | copy-start | bytes 98308
  0.0 3.8 %copy-start.2 = (bf16[128,128]{1,0:T(8,128)(2,1)S(1)}, bf16[128,128]{1,0:T(8,128)(2,1)}, u32[]{:S(2)}) copy-start(bf16[128,128]{1,0:T(8,128)(2,1)} %param.17) | copy-start | bytes 98308
  4.9 24.3 %copy-start.6 = (s32[8]{0:T(128)S(1)}, s32[8]{0:T(128)}, u32[]{:S(2)}) copy-start(s32[8]{0:T(128)} %param.20) | copy-start | bytes 100
  4.9 24.3 %copy-start.7 = (s32[8]{0:T(128)S(1)}, s32[8]{0:T(128)}, u32[]{:S(2)}) copy-start(s32[8]{0:T(128)} %param.21) | copy-start | bytes 100
  5.0 24.3 %copy-start.1 = (bf16[128,128]{1,0:T(8,128)(2,1)S(1)}, bf16[128,128]{1,0:T(8,128)(2,1)}, u32[]{:S(2)}) copy-start(bf16[128,128]{1,0:T(8,128)(2,1)} %param.19) | copy-start | bytes 98308
where the time goes:
time: 57 us; the launch traced here: 56.8 us
  blocking collectives  36.4 us (64%)
  matrix products  10.6 us (19%)
  other arithmetic  4.09 us (7%)
  local copies, waits for them, and re-layouts  3.88 us (7%)
  loops' own time  1.56 us (3%)
    all_gather x1, blocking collectives, local(): all_bias = lax.all_gather(local_bias, 'row', axis=1, tiled=True)  23.8 us
    all_to_all x1, blocking collectives, local(): lax.all_to_all(result, 'row', split_axis=1, concat_axis=0, tiled=True)  12.6 us
    dot_general x2, matrix products, one_block(): jnp.einsum('rhjk,rkhd->rjhd', weights, value, preferred_element_type=jnp....  7.26 us
    sub x2, matrix products, one_block(): raised = jnp.exp(scores - top)  1.69 us
    another operation x1, loops' own time, local(): blocks = lax.map(one_block, jnp.arange(length // block, dtype=jnp.int32))  1.56 us
    dynamic_slice x2, local copies, waits for them, and re-layouts, local(): blocks = lax.map(one_block, jnp.arange(length // block, dtype=jnp.int32))  1.33 us
    reduce_sum x1, other arithmetic, normalize(): spread = jnp.mean((values - center) ** 2, axis=-1, keepdims=True)  1.32 us
    convert_element_type x1, other arithmetic, normalize(): ((values - center) * lax.rsqrt(spread + 1e-05) * norm_gain).astype(jnp.bf...  1.29 us

commit v1 on v0

v1 whole, which is shorter than its diff:
```python
import functools
import math

import jax
import jax.numpy as jnp
from jax import lax
from jax.experimental import pallas as pl
from jax.experimental.pallas import tpu as pltpu
from jax.sharding import PartitionSpec as P

H = 4
LOG2E = math.log2(math.e)
MESH = pl.DeviceIdType.MESH
NT = (((1,), (1,)), ((), ()))


def other(index, step, count):
    if count & (count - 1):
        return lax.rem(index + step, count)
    result, bit = 0, 1
    while bit < count:
        a, b = index // bit % 2, step // bit % 2
        result = result + (a + b - 2 * a * b) * bit
        bit *= 2
    return result


def kernel(
    n,
    x_hbm,
    gain_hbm,
    wq_hbm,
    wk_hbm,
    wv_hbm,
    wg_hbm,
    wb_hbm,
    wo_hbm,
    start_ref,
    length_ref,
    out_ref,
    x_ref,
    gain_ref,
    wq_ref,
    wk_ref,
    wv_ref,
    wg_ref,
    wb_ref,
    wo_ref,
    wide_ref,
    bias_ref,
    score_ref,
    value_ref,
    sig_ref,
    gated_ref,
    send_ref,
    in_sem,
    bias_send,
    bias_recv,
    out_send,
    out_recv,
    own_sem,
):
    rows, width, channels = x_ref.shape
    head = channels // H
    chips = n // 2
    me = lax.axis_index("row")
    core, chip = me % 2, me // 2
    mate = me + 1 - 2 * core

    barrier = pltpu.get_barrier_semaphore()

    def greet(step, carry):
        pl.semaphore_signal(
            barrier, inc=1, device_id={"row": lax.rem(me + step, n)}, device_id_type=MESH
        )
        return carry

    lax.fori_loop(1, n, greet, 0)

    loads = [
        pltpu.make_async_copy(source, target, in_sem.at[at])
        for at, (source, target) in enumerate(
            (
                (x_hbm, x_ref),
                (gain_hbm, gain_ref),
                (wb_hbm, wb_ref),
                (wq_hbm, wq_ref),
                (wk_hbm, wk_ref),
                (wv_hbm, wv_ref),
                (wg_hbm, wg_ref),
                (wo_hbm, wo_ref),
            )
        )
    ]
    for load in loads:
        load.start()

    wide_ref[...] = jnp.zeros_like(wide_ref)
    loads[2].wait()
    wide_ref[:, :H] = wb_ref[...].astype(jnp.float32)
    bias_weight = wide_ref[...].T[:8].astype(jnp.bfloat16)
    loads[0].wait()
    loads[1].wait()
    gain = gain_ref[...]
    normed = []
    for i in range(rows):
        values = x_ref[i].astype(jnp.float32)
        center = jnp.mean(values, axis=-1, keepdims=True)
        values = values - center
        spread = jnp.mean(values * values, axis=-1, keepdims=True)
        row = (values * lax.rsqrt(spread + 1e-05) * gain).astype(jnp.bfloat16)
        x_ref[i] = row
        local = lax.dot_general(bias_weight, row, NT, preferred_element_type=jnp.float32)
        local = local * LOG2E
        for h in range(H):
            bias_ref[me, h, i : i + 1, :] = local[h : h + 1]

    pl.semaphore_wait(barrier, n - 1)

    def bias_copy(source, target, slot):
        return pltpu.make_async_remote_copy(
            src_ref=bias_ref.at[source],
            dst_ref=bias_ref.at[source],
            send_sem=bias_send.at[slot],
            recv_sem=bias_recv.at[source],
            device_id={"row": target},
            device_id_type=MESH,
        )

    def send_bias(at, carry):
        peer = other(chip, chips - 1 - at, chips) * 2
        for c in range(2):
            bias_copy(me, peer + c, peer + c).start()
        return carry

    lax.fori_loop(0, chips - 1, send_bias, 0)
    bias_copy(me, mate, mate).start()

    for load in loads[3:7]:
        load.wait()
    lane = lax.broadcasted_iota(jnp.int32, (1, channels), 1) // head
    masks = [(lane == h).astype(jnp.float32).astype(jnp.bfloat16) for h in range(H)]
    place = lax.broadcasted_iota(jnp.int32, (1, width), 1)
    factor = LOG2E / head**0.5

    def project(i):
        row = x_ref[i]

        def through(weight):
            return jnp.dot(row, weight[...], preferred_element_type=jnp.float32)

        query = through(wq_ref).astype(jnp.bfloat16)
        key = through(wk_ref).astype(jnp.bfloat16)
        value = through(wv_ref).astype(jnp.bfloat16)
        gate = through(wg_ref).astype(jnp.bfloat16).astype(jnp.float32)
        sig_ref[i] = jax.nn.sigmoid(gate)
        first = start_ref[i]
        valid = (place >= first) & (place < first + length_ref[i])
        for h in range(H):
            span = slice(h * width, (h + 1) * width)
            value_ref[i, span, :] = value * masks[h]
            part = lax.dot_general(
                query, key * masks[h], NT, preferred_element_type=jnp.float32
            )
            score_ref[i, :, span] = jnp.where(valid, part * factor, jnp.float32(-1e30))

    if width <= 128:
        for i in range(rows):
            project(i)
    else:
        pl.loop(0, rows)(project)
    loads[7].wait()

    both = 2 * rows

    def attend(first):
        columns = pl.ds(pl.multiple_of(first * rows, both), both)
        biases = [bias_ref[pl.ds(first, 2), h].reshape(both, width) for h in range(H)]
        for i in range(rows):
            parts = []
            for h in range(H):
                t = score_ref[i, columns, h * width : (h + 1) * width] + biases[h]
                raised = jnp.exp2(t - jnp.max(t, axis=-1, keepdims=True))
                total = jnp.sum(raised, axis=-1, keepdims=True)
                parts.append((raised * (1.0 / total)).astype(jnp.bfloat16))
            attended = jnp.dot(
                jnp.concatenate(parts, axis=1), value_ref[i], preferred_element_type=jnp.float32
            )
            gated_ref[i * both : (i + 1) * both, :] = (sig_ref[i, columns, :] * attended).astype(
                jnp.bfloat16
            )
        mixed = jnp.dot(gated_ref[...], wo_ref[...], preferred_element_type=jnp.float32)
        mixed = mixed.reshape(rows, both, channels)
        for c in range(2):
            send_ref[first + c] = mixed[:, c * rows : (c + 1) * rows, :].astype(jnp.bfloat16)

    def out_copy(source, target):
        return pltpu.make_async_remote_copy(
            src_ref=send_ref.at[target],
            dst_ref=out_ref.at[pl.ds(pl.multiple_of(source * rows, rows), rows)],
            send_sem=out_send.at[target],
            recv_sem=out_recv.at[source],
            device_id={"row": target},
            device_id_type=MESH,
        )

    bias_copy(mate, mate, mate).wait_recv()
    attend(chip * 2)
    own = pltpu.make_async_copy(
        send_ref.at[me], out_ref.at[pl.ds(pl.multiple_of(me * rows, rows), rows)], own_sem
    )
    own.start()
    out_copy(me, mate).start()

    def one_chip(step, carry):
        peer = other(chip, step, chips) * 2
        for c in range(2):
            bias_copy(peer + c, peer + c, peer + c).wait_recv()
        attend(peer)
        for c in range(2):
            out_copy(me, peer + c).start()
        return carry

    lax.fori_loop(1, chips, one_chip, 0)

    def finish(peer):
        bias_copy(me, peer, peer).wait_send()
        out_copy(me, peer).wait_send()
        out_copy(peer, peer).wait_recv()

    finish(mate)

    def finish_chip(step, carry):
        peer = other(chip, step, chips) * 2
        for c in range(2):
            finish(peer + c)
        return carry

    lax.fori_loop(1, chips, finish_chip, 0)
    own.wait()


def local(
    n, pair_map, norm_gain, w_query, w_key, w_value, w_gate, w_bias, w_output, window_start, key_length
):
    rows, width, channels = pair_map.shape
    anywhere = pl.BlockSpec(memory_space=pl.ANY)
    scalars = pl.BlockSpec(memory_space=pltpu.SMEM)
    weight = pltpu.VMEM((channels, channels), jnp.bfloat16)
    return pl.pallas_call(
        functools.partial(kernel, n),
        out_shape=jax.ShapeDtypeStruct((n * rows, width // n, channels), jnp.bfloat16),
        in_specs=[anywhere] * 8 + [scalars] * 2,
        out_specs=anywhere,
        scratch_shapes=[
            pltpu.VMEM((rows, width, channels), jnp.bfloat16),
            pltpu.VMEM((1, channels), jnp.float32),
            weight,
            weight,
            weight,
            weight,
            pltpu.VMEM((channels, H), jnp.bfloat16),
            weight,
            pltpu.VMEM((channels, channels), jnp.float32),
            pltpu.VMEM((n, H, rows, width), jnp.float32),
            pltpu.VMEM((rows, width, H * width), jnp.float32),
            pltpu.VMEM((rows, H * width, channels), jnp.bfloat16),
            pltpu.VMEM((rows, width, channels), jnp.float32),
            pltpu.VMEM((2 * rows * rows, channels), jnp.bfloat16),
            pltpu.VMEM((n, rows, width // n, channels), jnp.bfloat16),
            pltpu.SemaphoreType.DMA((8,)),
            pltpu.SemaphoreType.DMA((n,)),
            pltpu.SemaphoreType.DMA((n,)),
            pltpu.SemaphoreType.DMA((n,)),
            pltpu.SemaphoreType.DMA((n,)),
            pltpu.SemaphoreType.DMA,
        ],
        compiler_params=pltpu.CompilerParams(
            collective_id=0, has_side_effects=True, vmem_limit_bytes=60 * 1024 * 1024
        ),
        name="attend",
    )(
        pair_map,
        norm_gain.reshape(1, channels),
        w_query,
        w_key,
        w_value,
        w_gate,
        w_bias,
        w_output,
        window_start,
        key_length,
    )


def solution(mesh):
    return jax.shard_map(
        functools.partial(local, mesh.shape["row"]),
        mesh=mesh,
        in_specs=(
            P(("grp", "row"), None, None),
            P(),
            P(),
            P(),
            P(),
            P(),
            P(),
            P(),
            P(("grp", "row")),
            P(("grp", "row")),
        ),
        out_specs=P("grp", "row", None),
        check_vma=False,
    )
```

time: 57 us -> 25.2 us (0.44)
  blocking collectives: 36.4 us -> 0 us
  Pallas kernels: 0 us -> 21.9 us
  matrix products: 10.6 us -> 0 us
  other arithmetic: 4.09 us -> 0 us
  loops' own time: 1.56 us -> 0 us
  local copies, waits for them, and re-layouts: 3.88 us -> 3.08 us
    all_gather x1 -> x0, blocking collectives: 23.8 us -> none  [local(): all_bias = lax.all_gather(local_bias, 'row', axis=1, tiled=True)]
    pallas_call x0 -> x1, Pallas kernels: none -> 21.9 us  [local(): pl.pallas_call(functools.partial(kernel, n), out_shape=jax.ShapeDtypeStru...]
    all_to_all x1 -> x0, blocking collectives: 12.6 us -> none  [local(): lax.all_to_all(result, 'row', split_axis=1, concat_axis=0, tiled=True)]
    dot_general x8 -> x0, matrix products: 8.87 us -> none  [the longest x2 7.26 us: one_block(): jnp.einsum('rhjk,rkhd->rjhd', weights, value, preferred_element_type=jnp....]
    unnamed x21 -> x4, local copies, waits for them, and re-layouts: 0.25 us -> 3.08 us
    reduce_sum x2 -> x0, other arithmetic: 2.46 us -> none  [the longest x1 1.32 us: normalize(): spread = jnp.mean((values - center) ** 2, axis=-1, keepdims=True)]
    sub x2 -> x0, matrix products: 1.69 us -> none  [one_block(): raised = jnp.exp(scores - top)]
    dynamic_slice x8 -> x0, local copies, waits for them, and re-layouts: 1.67 us -> none  [the longest x2 1.33 us: local(): blocks = lax.map(one_block, jnp.arange(length // block, dtype=jnp.int32))]
where the time goes in v1:
time: 25.2 us; the launch traced here: 25 us
  Pallas kernels  21.9 us (87%)
  local copies, waits for them, and re-layouts  3.08 us (12%)
    pallas_call x1, Pallas kernels, local(): pl.pallas_call(functools.partial(kernel, n), out_shape=jax.ShapeDtypeStru...  21.9 us
    unnamed x4, local copies, waits for them, and re-layouts  3.08 us

profile of v1, /device:TPU:0, one launch (start us, length us, event | category | flops | bytes accessed | tf_op | source)
XLA Modules:
  0.0 25.0 jit_solution(637882523975434999)
XLA Ops:
  0.0 0.0 copy-start
  0.0 0.7 %copy-done = bf16[128,4]{0,1:T(4,128)(2,1)S(1)} copy-done((bf16[128,4]{0,1:T(4,128)(2,1)S(1)}, bf16[128,4]{0,1:T(4,128)(2,1)}, u32[]{:S(2)}) %copy-start) | copy-done | bytes 1048
  0.7 0.7 %copy.11.wb_hbm = bf16[128,4]{1,0:T(8,128)(2,1)} copy(bf16[128,4]{0,1:T(4,128)(2,1)S(1)} %copy-done) | data formatting | bytes 2048 | tf_op args[6]
  1.4 21.9 %attend.1 = bf16[128,8,128]{2,1,0:T(8,128)(2,1)} custom-call(bf16[8,128,128]{2,1,0:T(8,128)(2,1)} %x_hbm.1, f32[1,128]{1,0:T(1,128)} %bitcast.1, bf16[128,128]{1,0:T(8,128)(2,1)} %wq_hbm.1, bf16[128,128]{1,0:T(8,128)(2,1)} %wk_hbm.1, bf16[128,128]{1,0:T(8,128)(2,1)} %wv_hbm.1, bf16[128,128]{1,0:T(8,128)(2,1)} %wg_hbm.1, bf16[128,4]{1,0:T(8,128)(2,1)} %copy.11.wb_hbm, ...), custom_call_target="tpu_custom_call" | custom-call | tf_op jit(solution)/shard_map/attend/pallas_call | solution.py:250
  23.3 1.7 %copy.13 = bf16[128,8,128]{2,1,0:T(8,128)(2,1)} copy(bf16[128,8,128]{2,1,0:T(8,128)(2,1)} %attend.1) | data formatting | bytes 524288
Async XLA Ops:
  0.0 0.7 %copy-start = (bf16[128,4]{0,1:T(4,128)(2,1)S(1)}, bf16[128,4]{0,1:T(4,128)(2,1)}, u32[]{:S(2)}) copy-start(bf16[128,4]{0,1:T(4,128)(2,1)} %param.16) | copy-start | bytes 3076

commit v2 on v1

--- a/solution.py
+++ b/solution.py
@@ -46,7 +46,6 @@
     wg_ref,
     wb_ref,
     wo_ref,
-    wide_ref,
     bias_ref,
     score_ref,
     value_ref,
@@ -95,10 +94,8 @@
     for load in loads:
         load.start()
 
-    wide_ref[...] = jnp.zeros_like(wide_ref)
     loads[2].wait()
-    wide_ref[:, :H] = wb_ref[...].astype(jnp.float32)
-    bias_weight = wide_ref[...].T[:8].astype(jnp.bfloat16)
+    bias_weight = wb_ref[...]
     loads[0].wait()
     loads[1].wait()
     gain = gain_ref[...]
@@ -245,13 +242,16 @@
 ):
     rows, width, channels = pair_map.shape
     anywhere = pl.BlockSpec(memory_space=pl.ANY)
+    outside = pl.BlockSpec(memory_space=pltpu.HBM)
+    plane = rows * width * 4
+    grant = 4 * 1024 * 1024 + plane * (2 * H * width + 2 * H * channels + 4 * channels)
     scalars = pl.BlockSpec(memory_space=pltpu.SMEM)
     weight = pltpu.VMEM((channels, channels), jnp.bfloat16)
     return pl.pallas_call(
         functools.partial(kernel, n),
-        out_shape=jax.ShapeDtypeStruct((n * rows, width // n, channels), jnp.bfloat16),
-        in_specs=[anywhere] * 8 + [scalars] * 2,
-        out_specs=anywhere,
+        out_shape=pltpu.VMEM((n * rows, width // n, channels), jnp.bfloat16),
+        in_specs=[outside] * 8 + [scalars] * 2,
+        out_specs=pl.BlockSpec(memory_space=pltpu.VMEM),
         scratch_shapes=[
             pltpu.VMEM((rows, width, channels), jnp.bfloat16),
             pltpu.VMEM((1, channels), jnp.float32),
@@ -259,9 +259,8 @@
             weight,
             weight,
             weight,
-            pltpu.VMEM((channels, H), jnp.bfloat16),
-            weight,
-            pltpu.VMEM((channels, channels), jnp.float32),
+            pltpu.VMEM((H, channels), jnp.bfloat16),
+            weight,
             pltpu.VMEM((n, H, rows, width), jnp.float32),
             pltpu.VMEM((rows, width, H * width), jnp.float32),
             pltpu.VMEM((rows, H * width, channels), jnp.bfloat16),
@@ -276,7 +275,7 @@
             pltpu.SemaphoreType.DMA,
         ],
         compiler_params=pltpu.CompilerParams(
-            collective_id=0, has_side_effects=True, vmem_limit_bytes=60 * 1024 * 1024
+            collective_id=0, has_side_effects=True, vmem_limit_bytes=56 * 1024 * 1024
         ),
         name="attend",
     )(
@@ -286,7 +285,7 @@
         w_key,
         w_value,
         w_gate,
-        w_bias,
+        w_bias.T,
         w_output,
         window_start,
         key_length,

time: 25.2 us -> 22.6 us (0.90)
  local copies, waits for them, and re-layouts: 3.08 us -> 0.71 us
    unnamed x4 -> x1, local copies, waits for them, and re-layouts: 3.08 us -> 0.71 us
where the time goes in v2:
time: 22.6 us; the launch traced here: 22.4 us
  Pallas kernels  21.7 us (96%)
  local copies, waits for them, and re-layouts  0.71 us (3%)
    pallas_call x1, Pallas kernels, local(): pl.pallas_call(functools.partial(kernel, n), out_shape=pltpu.VMEM((n * ro...  21.7 us
    unnamed x1, local copies, waits for them, and re-layouts  0.71 us

profile of v2, /device:TPU:0, one launch (start us, length us, event | category | flops | bytes accessed | tf_op | source)
XLA Modules:
  0.0 22.4 jit_solution(5280374313684638511)
XLA Ops:
  0.0 21.7 %attend.1 = bf16[128,8,128]{2,1,0:T(8,128)(2,1)S(1)} custom-call(bf16[8,128,128]{2,1,0:T(8,128)(2,1)} %x_hbm.1, f32[1,128]{1,0:T(1,128)} %bitcast.3, bf16[128,128]{1,0:T(8,128)(2,1)} %wq_hbm.1, bf16[128,128]{1,0:T(8,128)(2,1)} %wk_hbm.1, bf16[128,128]{1,0:T(8,128)(2,1)} %wv_hbm.1, bf16[128,128]{1,0:T(8,128)(2,1)} %wg_hbm.1, bf16[4,128]{1,0:T(4,128)(2,1)} %bitcast.2, ...), custom_call_target="tpu_custom_call" | custom-call | tf_op jit(solution)/shard_map/attend/pallas_call | solution.py:250
  21.7 0.7 %copy.12 = bf16[128,8,128]{2,1,0:T(8,128)(2,1)} copy(bf16[128,8,128]{2,1,0:T(8,128)(2,1)S(1)} %attend.1) | data formatting | bytes 524288

commit v3 on v2

--- a/solution.py
+++ b/solution.py
@@ -35,8 +35,8 @@
     wg_hbm,
     wb_hbm,
     wo_hbm,
-    start_ref,
-    length_ref,
+    start_hbm,
+    length_hbm,
     out_ref,
     x_ref,
     gain_ref,
@@ -48,16 +48,18 @@
     wo_ref,
     bias_ref,
     score_ref,
+    key_ref,
     value_ref,
     sig_ref,
     gated_ref,
     send_ref,
+    start_ref,
+    length_ref,
     in_sem,
     bias_send,
     bias_recv,
     out_send,
     out_recv,
-    own_sem,
 ):
     rows, width, channels = x_ref.shape
     head = channels // H
@@ -68,36 +70,45 @@
 
     barrier = pltpu.get_barrier_semaphore()
 
-    def greet(step, carry):
-        pl.semaphore_signal(
-            barrier, inc=1, device_id={"row": lax.rem(me + step, n)}, device_id_type=MESH
-        )
+    def greet(at, carry):
+        peer = other(chip, chips - 1 - at, chips) * 2
+        for c in range(2):
+            pl.semaphore_signal(barrier, inc=1, device_id={"row": peer + c}, device_id_type=MESH)
         return carry
 
-    lax.fori_loop(1, n, greet, 0)
-
-    loads = [
-        pltpu.make_async_copy(source, target, in_sem.at[at])
-        for at, (source, target) in enumerate(
+    lax.fori_loop(0, chips - 1, greet, 0, unroll=chips <= 16)
+    pl.semaphore_signal(barrier, inc=1, device_id={"row": mate}, device_id_type=MESH)
+
+    def load(pairs, slot):
+        copies = [pltpu.make_async_copy(source, target, in_sem.at[slot]) for source, target in pairs]
+        for copy in copies:
+            copy.start()
+        return copies
+
+    def arrived(copies):
+        for copy in copies:
+            copy.wait()
+
+    first_in = load([(x_hbm, x_ref)], 0), load([(gain_hbm, gain_ref)], 1), load([(wb_hbm, wb_ref)], 2)
+    weights_in = [
+        load([pair], 3 + at)
+        for at, pair in enumerate(
             (
-                (x_hbm, x_ref),
-                (gain_hbm, gain_ref),
-                (wb_hbm, wb_ref),
                 (wq_hbm, wq_ref),
                 (wk_hbm, wk_ref),
                 (wv_hbm, wv_ref),
                 (wg_hbm, wg_ref),
                 (wo_hbm, wo_ref),
+                (start_hbm, start_ref),
+                (length_hbm, length_ref),
             )
         )
     ]
-    for load in loads:
-        load.start()
-
-    loads[2].wait()
+
+    key_ref[...] = jnp.zeros_like(key_ref)
+    for copies in first_in:
+        arrived(copies)
     bias_weight = wb_ref[...]
-    loads[0].wait()
-    loads[1].wait()
     gain = gain_ref[...]
     normed = []
     for i in range(rows):
@@ -114,27 +125,30 @@
 
     pl.semaphore_wait(barrier, n - 1)
 
-    def bias_copy(source, target, slot):
+    def bias_copy(source, target):
         return pltpu.make_async_remote_copy(
             src_ref=bias_ref.at[source],
             dst_ref=bias_ref.at[source],
-            send_sem=bias_send.at[slot],
+            send_sem=bias_send,
             recv_sem=bias_recv.at[source],
             device_id={"row": target},
             device_id_type=MESH,
         )
 
     def send_bias(at, carry):
-        peer = other(chip, chips - 1 - at, chips) * 2
-        for c in range(2):
-            bias_copy(me, peer + c, peer + c).start()
+        bias_copy(me, other(chip, chips - 1 - at, chips) * 2 + core).start()
         return carry
 
-    lax.fori_loop(0, chips - 1, send_bias, 0)
-    bias_copy(me, mate, mate).start()
-
-    for load in loads[3:7]:
-        load.wait()
+    lax.fori_loop(0, chips - 1, send_bias, 0, unroll=chips <= 16)
+    bias_copy(me, mate).start()
+
+    def hand_over(step):
+        source = other(chip, step, chips) * 2 + core
+        bias_copy(source, mate).wait_recv()
+        bias_copy(source, mate).start()
+
+    for copies in weights_in:
+        arrived(copies)
     lane = lax.broadcasted_iota(jnp.int32, (1, channels), 1) // head
     masks = [(lane == h).astype(jnp.float32).astype(jnp.bfloat16) for h in range(H)]
     place = lax.broadcasted_iota(jnp.int32, (1, width), 1)
@@ -153,20 +167,20 @@
         sig_ref[i] = jax.nn.sigmoid(gate)
         first = start_ref[i]
         valid = (place >= first) & (place < first + length_ref[i])
+        turned = key.T
         for h in range(H):
             span = slice(h * width, (h + 1) * width)
+            part = slice(h * head, (h + 1) * head)
             value_ref[i, span, :] = value * masks[h]
-            part = lax.dot_general(
-                query, key * masks[h], NT, preferred_element_type=jnp.float32
-            )
-            score_ref[i, :, span] = jnp.where(valid, part * factor, jnp.float32(-1e30))
+            key_ref[i, part, span] = turned[part]
+            scores = jnp.dot(query, key_ref[i, :, span], preferred_element_type=jnp.float32)
+            score_ref[i, :, span] = jnp.where(valid, scores * factor, jnp.float32(-1e30))
 
     if width <= 128:
         for i in range(rows):
             project(i)
     else:
         pl.loop(0, rows)(project)
-    loads[7].wait()
 
     both = 2 * rows
 
@@ -188,69 +202,94 @@
             )
         mixed = jnp.dot(gated_ref[...], wo_ref[...], preferred_element_type=jnp.float32)
         mixed = mixed.reshape(rows, both, channels)
-        for c in range(2):
-            send_ref[first + c] = mixed[:, c * rows : (c + 1) * rows, :].astype(jnp.bfloat16)
-
-    def out_copy(source, target):
+        return mixed.astype(jnp.bfloat16)
+
+    def out_copy(target):
         return pltpu.make_async_remote_copy(
             src_ref=send_ref.at[target],
-            dst_ref=out_ref.at[pl.ds(pl.multiple_of(source * rows, rows), rows)],
-            send_sem=out_send.at[target],
-            recv_sem=out_recv.at[source],
+            dst_ref=out_ref.at[pl.ds(pl.multiple_of(me * rows, rows), rows)],
+            send_sem=out_send,
+            recv_sem=out_recv,
             device_id={"row": target},
             device_id_type=MESH,
         )
 
-    bias_copy(mate, mate, mate).wait_recv()
-    attend(chip * 2)
-    own = pltpu.make_async_copy(
-        send_ref.at[me], out_ref.at[pl.ds(pl.multiple_of(me * rows, rows), rows)], own_sem
+    def send_chip(mixed, first, mine):
+        for c in range(2):
+            send_ref[first + c] = mixed[:, c * rows : (c + 1) * rows, :]
+        if mine:
+            out_ref[pl.ds(pl.multiple_of(me * rows, rows), rows)] = send_ref[me]
+            out_copy(mate).start()
+        else:
+            for c in range(2):
+                out_copy(first + c).start()
+
+    def own_chip():
+        bias_copy(mate, mate).wait_recv()
+        send_chip(attend(chip * 2), chip * 2, True)
+
+    def one_chip(step):
+        peer = other(chip, step, chips) * 2
+        bias_copy(peer + 1 - core, mate).wait_recv()
+        send_chip(attend(peer), peer, False)
+
+    if chips == 8:
+        for step in (1, 2, 3):
+            hand_over(step)
+        own_chip()
+        one_chip(1)
+        for step in (4, 5):
+            hand_over(step)
+        one_chip(2)
+        for step in (6, 7):
+            hand_over(step)
+        for step in (4, 5, 6, 7, 3):
+            one_chip(step)
+    else:
+        hand_over(1)
+        own_chip()
+
+        def answer(step, carry):
+            @pl.when(step < chips - 1)
+            def _():
+                hand_over(step + 1)
+
+            one_chip(step)
+            return carry
+
+        lax.fori_loop(1, chips, answer, 0)
+
+    rest = pltpu.make_async_remote_copy(
+        src_ref=bias_ref.at[pl.ds(0, n - 1)],
+        dst_ref=bias_ref.at[pl.ds(0, n - 1)],
+        send_sem=bias_send,
+        recv_sem=bias_recv.at[me],
+        device_id={"row": mate},
+        device_id_type=MESH,
     )
-    own.start()
-    out_copy(me, mate).start()
-
-    def one_chip(step, carry):
-        peer = other(chip, step, chips) * 2
-        for c in range(2):
-            bias_copy(peer + c, peer + c, peer + c).wait_recv()
-        attend(peer)
-        for c in range(2):
-            out_copy(me, peer + c).start()
-        return carry
-
-    lax.fori_loop(1, chips, one_chip, 0)
-
-    def finish(peer):
-        bias_copy(me, peer, peer).wait_send()
-        out_copy(me, peer).wait_send()
-        out_copy(peer, peer).wait_recv()
-
-    finish(mate)
-
-    def finish_chip(step, carry):
-        peer = other(chip, step, chips) * 2
-        for c in range(2):
-            finish(peer + c)
-        return carry
-
-    lax.fori_loop(1, chips, finish_chip, 0)
-    own.wait()
+    rest.wait_send()
+    rest = pltpu.make_async_remote_copy(
+        src_ref=send_ref.at[pl.ds(0, n - 1)],
+        dst_ref=out_ref.at[pl.ds(0, (n - 1) * rows)],
+        send_sem=out_send,
+        recv_sem=out_recv,
+        device_id={"row": mate},
+        device_id_type=MESH,
+    )
+    rest.wait_send()
+    rest.wait_recv()
 
 
 def local(
     n, pair_map, norm_gain, w_query, w_key, w_value, w_gate, w_bias, w_output, window_start, key_length
 ):
     rows, width, channels = pair_map.shape
-    anywhere = pl.BlockSpec(memory_space=pl.ANY)
     outside = pl.BlockSpec(memory_space=pltpu.HBM)
-    plane = rows * width * 4
-    grant = 4 * 1024 * 1024 + plane * (2 * H * width + 2 * H * channels + 4 * channels)
-    scalars = pl.BlockSpec(memory_space=pltpu.SMEM)
     weight = pltpu.VMEM((channels, channels), jnp.bfloat16)
     return pl.pallas_call(
         functools.partial(kernel, n),
         out_shape=pltpu.VMEM((n * rows, width // n, channels), jnp.bfloat16),
-        in_specs=[outside] * 8 + [scalars] * 2,
+        in_specs=[outside] * 10,
         out_specs=pl.BlockSpec(memory_space=pltpu.VMEM),
         scratch_shapes=[
             pltpu.VMEM((rows, width, channels), jnp.bfloat16),
@@ -263,15 +302,17 @@
             weight,
             pltpu.VMEM((n, H, rows, width), jnp.float32),
             pltpu.VMEM((rows, width, H * width), jnp.float32),
+            pltpu.VMEM((rows, channels, H * width), jnp.bfloat16),
             pltpu.VMEM((rows, H * width, channels), jnp.bfloat16),
             pltpu.VMEM((rows, width, channels), jnp.float32),
             pltpu.VMEM((2 * rows * rows, channels), jnp.bfloat16),
             pltpu.VMEM((n, rows, width // n, channels), jnp.bfloat16),
-            pltpu.SemaphoreType.DMA((8,)),
+            pltpu.SMEM((rows,), jnp.int32),
+            pltpu.SMEM((rows,), jnp.int32),
+            pltpu.SemaphoreType.DMA((10,)),
+            pltpu.SemaphoreType.DMA,
             pltpu.SemaphoreType.DMA((n,)),
-            pltpu.SemaphoreType.DMA((n,)),
-            pltpu.SemaphoreType.DMA((n,)),
-            pltpu.SemaphoreType.DMA((n,)),
+            pltpu.SemaphoreType.DMA,
             pltpu.SemaphoreType.DMA,
         ],
         compiler_params=pltpu.CompilerParams(

time: 22.6 us -> 20.6 us (0.912)
  Pallas kernels: 21.7 us -> 19.7 us
    pallas_call x1, Pallas kernels: 21.7 us -> 19.7 us  [local(): pl.pallas_call(functools.partial(kernel, n), out_shape=pltpu.VMEM((n * ro...]
where the time goes in v3:
time: 20.6 us; the launch traced here: 20.4 us
  Pallas kernels  19.7 us (96%)
  local copies, waits for them, and re-layouts  0.71 us (3%)
    pallas_call x1, Pallas kernels, local(): pl.pallas_call(functools.partial(kernel, n), out_shape=pltpu.VMEM((n * ro...  19.7 us
    unnamed x1, local copies, waits for them, and re-layouts  0.71 us

profile of v3, /device:TPU:0, one launch (start us, length us, event | category | flops | bytes accessed | tf_op | source)
XLA Modules:
  0.0 20.4 jit_solution(1590037435488454628)
XLA Ops:
  0.0 19.7 %attend.1 = bf16[128,8,128]{2,1,0:T(8,128)(2,1)S(1)} custom-call(bf16[8,128,128]{2,1,0:T(8,128)(2,1)} %x_hbm.1, f32[1,128]{1,0:T(1,128)} %bitcast.3, bf16[128,128]{1,0:T(8,128)(2,1)} %wq_hbm.1, bf16[128,128]{1,0:T(8,128)(2,1)} %wk_hbm.1, bf16[128,128]{1,0:T(8,128)(2,1)} %wv_hbm.1, bf16[128,128]{1,0:T(8,128)(2,1)} %wg_hbm.1, bf16[4,128]{1,0:T(4,128)(2,1)} %bitcast.2, ...), custom_call_target="tpu_custom_call" | custom-call | tf_op jit(solution)/shard_map/attend/pallas_call | solution.py:289
  19.7 0.7 %copy.12 = bf16[128,8,128]{2,1,0:T(8,128)(2,1)} copy(bf16[128,8,128]{2,1,0:T(8,128)(2,1)S(1)} %attend.1) | data formatting | bytes 524288

commit v4 on v3

--- a/solution.py
+++ b/solution.py
@@ -48,7 +48,6 @@
     wo_ref,
     bias_ref,
     score_ref,
-    key_ref,
     value_ref,
     sig_ref,
     gated_ref,
@@ -68,6 +67,17 @@
     core, chip = me % 2, me // 2
     mate = me + 1 - 2 * core
 
+    def load(pairs, slot):
+        copies = [pltpu.make_async_copy(source, target, in_sem.at[slot]) for source, target in pairs]
+        for copy in copies:
+            copy.start()
+        return copies
+
+    def arrived(copies):
+        for copy in copies:
+            copy.wait()
+
+    first_in = load([(x_hbm, x_ref)], 0), load([(gain_hbm, gain_ref)], 1), load([(wb_hbm, wb_ref)], 2)
     barrier = pltpu.get_barrier_semaphore()
 
     def greet(at, carry):
@@ -79,17 +89,6 @@
     lax.fori_loop(0, chips - 1, greet, 0, unroll=chips <= 16)
     pl.semaphore_signal(barrier, inc=1, device_id={"row": mate}, device_id_type=MESH)
 
-    def load(pairs, slot):
-        copies = [pltpu.make_async_copy(source, target, in_sem.at[slot]) for source, target in pairs]
-        for copy in copies:
-            copy.start()
-        return copies
-
-    def arrived(copies):
-        for copy in copies:
-            copy.wait()
-
-    first_in = load([(x_hbm, x_ref)], 0), load([(gain_hbm, gain_ref)], 1), load([(wb_hbm, wb_ref)], 2)
     weights_in = [
         load([pair], 3 + at)
         for at, pair in enumerate(
@@ -105,16 +104,15 @@
         )
     ]
 
-    key_ref[...] = jnp.zeros_like(key_ref)
     for copies in first_in:
         arrived(copies)
     bias_weight = wb_ref[...]
     gain = gain_ref[...]
-    normed = []
+    ones = jnp.ones((channels, channels), jnp.bfloat16)
     for i in range(rows):
-        values = x_ref[i].astype(jnp.float32)
-        center = jnp.mean(values, axis=-1, keepdims=True)
-        values = values - center
+        row = x_ref[i]
+        center = jnp.dot(row, ones, preferred_element_type=jnp.float32) * (1.0 / channels)
+        values = row.astype(jnp.float32) - center
         spread = jnp.mean(values * values, axis=-1, keepdims=True)
         row = (values * lax.rsqrt(spread + 1e-05) * gain).astype(jnp.bfloat16)
         x_ref[i] = row
@@ -135,11 +133,20 @@
             device_id_type=MESH,
         )
 
-    def send_bias(at, carry):
+    near = chips // 2
+
+    def send_far(at, carry):
         bias_copy(me, other(chip, chips - 1 - at, chips) * 2 + core).start()
         return carry
 
-    lax.fori_loop(0, chips - 1, send_bias, 0, unroll=chips <= 16)
+    def send_near(at, carry):
+        peer = other(chip, near - 1 - at, chips) * 2
+        bias_copy(me, peer).start()
+        bias_copy(me, peer + 1).start()
+        return carry
+
+    lax.fori_loop(0, chips - near, send_far, 0, unroll=chips <= 16)
+    lax.fori_loop(0, near - 1, send_near, 0, unroll=chips <= 16)
     bias_copy(me, mate).start()
 
     def hand_over(step):
@@ -167,14 +174,13 @@
         sig_ref[i] = jax.nn.sigmoid(gate)
         first = start_ref[i]
         valid = (place >= first) & (place < first + length_ref[i])
-        turned = key.T
         for h in range(H):
             span = slice(h * width, (h + 1) * width)
-            part = slice(h * head, (h + 1) * head)
             value_ref[i, span, :] = value * masks[h]
-            key_ref[i, part, span] = turned[part]
-            scores = jnp.dot(query, key_ref[i, :, span], preferred_element_type=jnp.float32)
-            score_ref[i, :, span] = jnp.where(valid, scores * factor, jnp.float32(-1e30))
+            part = lax.dot_general(
+                query, key * masks[h], NT, preferred_element_type=jnp.float32
+            )
+            score_ref[i, :, span] = jnp.where(valid, part * factor, jnp.float32(-1e30))
 
     if width <= 128:
         for i in range(rows):
@@ -224,40 +230,38 @@
             for c in range(2):
                 out_copy(first + c).start()
 
-    def own_chip():
-        bias_copy(mate, mate).wait_recv()
-        send_chip(attend(chip * 2), chip * 2, True)
-
     def one_chip(step):
+        peer = other(chip, step, chips) * 2
+        for c in range(2):
+            bias_copy(peer + c, mate).wait_recv()
+        send_chip(attend(peer), peer, False)
+
+    def far_chip(step):
         peer = other(chip, step, chips) * 2
         bias_copy(peer + 1 - core, mate).wait_recv()
         send_chip(attend(peer), peer, False)
 
-    if chips == 8:
-        for step in (1, 2, 3):
+    bias_copy(mate, mate).wait_recv()
+    send_chip(attend(chip * 2), chip * 2, True)
+    if chips <= 8:
+        for step in range(1, near - 1):
+            one_chip(step)
+        hand_over(near)
+        one_chip(near - 1)
+        for step in range(near + 1, chips):
             hand_over(step)
-        own_chip()
-        one_chip(1)
-        for step in (4, 5):
+            far_chip(step - 1)
+    else:
+        pl.loop(1, near - 1)(one_chip)
+        hand_over(near)
+        one_chip(near - 1)
+
+        @pl.loop(near + 1, chips)
+        def _(step):
             hand_over(step)
-        one_chip(2)
-        for step in (6, 7):
-            hand_over(step)
-        for step in (4, 5, 6, 7, 3):
-            one_chip(step)
-    else:
-        hand_over(1)
-        own_chip()
-
-        def answer(step, carry):
-            @pl.when(step < chips - 1)
-            def _():
-                hand_over(step + 1)
-
-            one_chip(step)
-            return carry
-
-        lax.fori_loop(1, chips, answer, 0)
+            far_chip(step - 1)
+
+    far_chip(chips - 1)
 
     rest = pltpu.make_async_remote_copy(
         src_ref=bias_ref.at[pl.ds(0, n - 1)],
@@ -302,7 +306,6 @@
             weight,
             pltpu.VMEM((n, H, rows, width), jnp.float32),
             pltpu.VMEM((rows, width, H * width), jnp.float32),
-            pltpu.VMEM((rows, channels, H * width), jnp.bfloat16),
             pltpu.VMEM((rows, H * width, channels), jnp.bfloat16),
             pltpu.VMEM((rows, width, channels), jnp.float32),
             pltpu.VMEM((2 * rows * rows, channels), jnp.bfloat16),

time: 20.6 us -> 20.4 us (level)
  no operation moved by 1% of the time
where the time goes in v4:
time: 20.4 us; the launch traced here: 20.2 us
  Pallas kernels  19.5 us (96%)
  local copies, waits for them, and re-layouts  0.71 us (3%)
    pallas_call x1, Pallas kernels, local(): pl.pallas_call(functools.partial(kernel, n), out_shape=pltpu.VMEM((n * ro...  19.5 us
    unnamed x1, local copies, waits for them, and re-layouts  0.71 us

profile of v4, /device:TPU:0, one launch (start us, length us, event | category | flops | bytes accessed | tf_op | source)
XLA Modules:
  0.0 20.2 jit_solution(8113043805249846891)
XLA Ops:
  0.0 19.5 %attend.1 = bf16[128,8,128]{2,1,0:T(8,128)(2,1)S(1)} custom-call(bf16[8,128,128]{2,1,0:T(8,128)(2,1)} %x_hbm.1, f32[1,128]{1,0:T(1,128)} %bitcast.3, bf16[128,128]{1,0:T(8,128)(2,1)} %wq_hbm.1, bf16[128,128]{1,0:T(8,128)(2,1)} %wk_hbm.1, bf16[128,128]{1,0:T(8,128)(2,1)} %wv_hbm.1, bf16[128,128]{1,0:T(8,128)(2,1)} %wg_hbm.1, bf16[4,128]{1,0:T(4,128)(2,1)} %bitcast.2, ...), custom_call_target="tpu_custom_call" | custom-call | tf_op jit(solution)/shard_map/attend/pallas_call | solution.py:293
  19.5 0.7 %copy.12 = bf16[128,8,128]{2,1,0:T(8,128)(2,1)} copy(bf16[128,8,128]{2,1,0:T(8,128)(2,1)S(1)} %attend.1) | data formatting | bytes 524288
